TPU v7x, 32 devices: a whole 2x2x4 slice. The times are simulated.
32 devices in a mesh: band: 2 (over x), tm: 16 (over z, y, core).
Axes of the slice: x: 2, y: 2, z: 4, core: 2. Of those that a mesh axis runs over, the one named last changes fastest.
Arguments:
- voltages: bfloat16 [65536, 2048], P(('band', 'tm')), parts along dimension 0, may hold values from -6 to 6
- panel_map: int32 [2048], replicated, may hold values from 0 to 2047, each once
- block_list: int32 [16, 2], replicated, may hold values from 0 to 15, as said below
Outputs:
- visibilities: float32 [32, 2, 256, 128, 128], P('band', None, 'tm'), parts along dimension 0
There are 2 independent parts, one for each index of `band`. A program takes and returns all parts, laid end to end along the dimension named above; an argument that names none is the same for every part. Nothing has to cross between parts.
Inputs may be any that keep to these rules, and one draw needn't show every extreme that they name: `block_list`: each row is a pair of panel numbers; the list names exactly 8 distinct panels, among them panel 0 and panel 16 - 1, every one of them in its first column.
All inputs are finite; a program needn't handle non-finite values.
Results may differ from a plain program's by a relative error of at most 0.0064.
Values may be sent and summed in bfloat16 or wider, within the bound.
No kernel may reach another device: no remote copies, remote signals or barrier semaphores. Data moves between devices by JAX's collectives and lax.ppermute only.
A program may use at most 128 MiB of HBM per device.

v0:
```python
import jax
import jax.numpy as jnp
from jax import lax
from jax.sharding import PartitionSpec as P

CHANNELS = 256
TAPS = 4
PANEL = 128


def from_behind(block, axis, distance):
    devices = range(lax.axis_size(axis))
    route = [(i - distance, i) for i in devices if i - distance in devices]
    return lax.ppermute(block, axis, route)


def filter_taps(taps, frame):
    length = taps * frame
    place = jnp.arange(length).astype(jnp.float32)
    middle = (length - 1) / 2.0
    window = 0.5 - 0.5 * jnp.cos(2.0 * jnp.pi * (place + 0.5) / length)
    shape_h = jnp.sinc((place - middle) / frame) * window
    shape_h = shape_h / jnp.sqrt(jnp.sum(shape_h * shape_h))
    return shape_h.reshape(taps, frame).astype(jnp.float32)


def dft_table(channels):
    frame = 2 * channels
    rows_k = jnp.arange(channels, dtype=jnp.int32)[:, None]
    cols_n = jnp.arange(frame, dtype=jnp.int32)[None, :]
    phase = (rows_k * cols_n % frame).astype(jnp.float32) * (2.0 * jnp.pi / frame)
    return jnp.concatenate([jnp.cos(phase), -jnp.sin(phase)], axis=0).astype(jnp.bfloat16)


def body(voltages, panel_map, block_list):
    frame = 2 * CHANNELS
    spec_dev = voltages.shape[0] // frame
    groups = lax.axis_size("tm")
    band_dev = CHANNELS // groups
    panel_rows = panel_map.reshape(-1, PANEL)
    columns = panel_rows[block_list]
    width = voltages.shape[1]
    frames = voltages.reshape(spec_dev, frame, width)
    earlier = from_behind(frames[spec_dev - (TAPS - 1) :], "tm", 1)
    padded = jnp.concatenate([earlier, frames], axis=0)
    coeff = filter_taps(TAPS, frame)
    filtered = jnp.zeros((spec_dev, frame, width), jnp.float32)
    for tap in range(TAPS):
        filtered = filtered + coeff[tap][None, :, None] * padded[tap : tap + spec_dev].astype(
            jnp.float32
        )
    filtered = filtered.astype(jnp.bfloat16)
    table = dft_table(CHANNELS)
    spectra = jnp.einsum("kn,sni->ski", table, filtered, preferred_element_type=jnp.float32)
    spectra = spectra.astype(jnp.bfloat16).reshape(spec_dev, 2, groups, band_dev, width)
    data = lax.all_to_all(spectra, "tm", split_axis=2, concat_axis=0, tiled=True)[:, :, 0]
    total = data.shape[0]
    first = data[:, :, :, columns[:, 0]]
    second = data[:, :, :, columns[:, 1]]
    flipped = jnp.stack([first[:, 1], -first[:, 0]], axis=1)
    real_part = jnp.einsum("sckbi,sckbj->bkij", first, second, preferred_element_type=jnp.float32)
    imag_part = jnp.einsum("sckbi,sckbj->bkij", flipped, second, preferred_element_type=jnp.float32)
    return jnp.stack([real_part, imag_part], axis=1) / total


def solution(mesh):
    in_specs = (P(("band", "tm"), None), P(), P())
    out_specs = P("band", None, "tm", None, None)
    return jax.shard_map(body, mesh=mesh, in_specs=in_specs, out_specs=out_specs, check_vma=False)
```

profile of v0, /device:TPU:13, one launch (start us, length us, event | category | flops | bytes accessed | tf_op | source)
XLA Modules:
  0.0 472.7 jit_solution(12410593673535821267)
XLA Ops:
  0.0 0.0 copy-start
  0.0 6.6 %slice.44 = bf16[1536,2048]{1,0:T(8,128)(2,1)} slice(bf16[2048,2048]{1,0:T(8,128)(2,1)} %param.3), slice={[512:2048], [0:2048]} | slice | bytes 12582912 | tf_op jit(solution)/shard_map/slice | solution.py:44
  6.6 3.7 collective-permute-start
  10.3 0.6 multiply_reduce_fusion
  11.6 0.1 broadcast_divide_fusion
  11.6 2.2 negate_convert_fusion
  13.8 64.7 %collective-permute-done = bf16[3,512,2048]{2,1,0:T(8,128)(2,1)} collective-permute-done((bf16[3,512,2048]{2,1,0:T(8,128)(2,1)}, bf16[3,512,2048]{2,1,0:T(8,128)(2,1)}, u32[]{:S(2)}, u32[]{:S(2)}) %collective-permute-start) | collective-permute-done | bytes 6291488 | tf_op jit(solution)/shard_map/ppermute | solution.py:14
  78.5 17.1 %fusion.6 = bf16[4,2048,512]{1,2,0:T(8,128)(2,1)} fusion(bf16[4,512,2048]{2,1,0:T(8,128)(2,1)} %bitcast.51, bf16[3,512,2048]{2,1,0:T(8,128)(2,1)} %collective-permute-done, f32[512]{0:T(512)S(1)} %get-tuple-element.10, f32[512]{0:T(512)S(1)} %get-tuple-element.11, f32[512]{0:T(512)S(1)} %get-tuple-element.12, f32[512]{0:T(512)S(1)} %get-tuple-element.9, ...), kind=kOutput, calls=%fused_computation.18 | convolution fusion | flops 4388290560 | bytes 23601152 | tf_op jit(solution)/shard_map/kn,sni->ski/dot_general | solution.py:54
  95.6 0.0 copy-start.2
  95.6 8.3 %copy.7 = bf16[4,2,16,16,2048]{4,3,1,0,2:T(8,128)(2,1)} copy(bf16[4,2,16,16,2048]{4,3,2,1,0:T(8,128)(2,1)} %bitcast.50) | data formatting | bytes 16777216 | tf_op jit(solution)/shard_map/reshape | solution.py:55
  103.9 7.2 %all-to-all-start = ((bf16[4,2,16,16,2048]{4,3,1,0,2:T(8,128)(2,1)}), bf16[4,2,16,16,2048]{4,3,1,0,2:T(8,128)(2,1)}, u32[]{:S(2)}, u32[]{:S(2)}) async-start(bf16[4,2,16,16,2048]{4,3,1,0,2:T(8,128)(2,1)} %copy.7), calls=%async_computation | async-start | bytes 16777216 | tf_op jit(solution)/shard_map/all_to_all | solution.py:56
  111.1 0.0 copy-done.2
  111.1 0.1 copy.8
  111.2 0.1 reshape.85
  111.3 0.0 copy-done
  111.3 0.6 gather_fusion
  112.0 181.5 %all-to-all-done = bf16[4,2,16,16,2048]{4,3,1,0,2:T(8,128)(2,1)} async-done(((bf16[4,2,16,16,2048]{4,3,1,0,2:T(8,128)(2,1)}), bf16[4,2,16,16,2048]{4,3,1,0,2:T(8,128)(2,1)}, u32[]{:S(2)}, u32[]{:S(2)}) %all-to-all-start) | async-done | bytes 8388640 | tf_op jit(solution)/shard_map/all_to_all | solution.py:56
  293.5 26.8 %copy.9 = bf16[64,2,16,2048]{0,2,3,1:T(8,128)(2,1)} copy(bf16[64,2,16,2048]{3,2,1,0:T(8,128)(2,1)} %bitcast.7) | data formatting | bytes 16777216 | tf_op jit(solution)/shard_map/squeeze | solution.py:56
  320.3 25.9 %gather_fusion.2 = bf16[2048,64,2,16]{1,3,2,0:T(8,128)(2,1)} fusion(bf16[64,2,16,2048]{0,2,3,1:T(8,128)(2,1)} %copy.9, s32[2048]{0:T(1024)S(1)} %fusion.26), kind=kCustom, calls=%fused_computation.2 | custom fusion | bytes 16785408 | tf_op jit(solution)/shard_map/gather | solution.py:59
  346.2 25.9 %gather_fusion.1 = bf16[2048,64,2,16]{1,3,2,0:T(8,128)(2,1)} fusion(bf16[64,2,16,2048]{0,2,3,1:T(8,128)(2,1)} %copy.9, s32[2048]{0:T(1024)S(1)} %fusion.24), kind=kCustom, calls=%fused_computation.1 | custom fusion | bytes 16785408 | tf_op jit(solution)/shard_map/gather | solution.py:58
  372.0 21.0 %copy.11 = bf16[16,128,64,2,16]{1,2,3,4,0:T(8,128)(2,1)} copy(bf16[16,128,64,2,16]{2,4,3,1,0:T(8,128)(2,1)} %bitcast.49) | data formatting | bytes 16777216 | tf_op jit(solution)/shard_map/gather | solution.py:58
  393.0 21.1 %copy.15 = bf16[64,2,16,16,128]{4,0,1,2,3:T(8,128)(2,1)} copy(bf16[64,2,16,16,128]{0,2,1,4,3:T(8,128)(2,1)} %bitcast.48) | data formatting | bytes 16777216 | tf_op jit(solution)/shard_map/gather | solution.py:59
  414.1 5.8 %fusion.35 = (bf16[64,1,16,16,128]{4,0,1,2,3:T(8,128)(2,1)}, bf16[64,1,16,16,128]{4,0,1,2,3:T(8,128)(2,1)}) fusion(bf16[64,2,16,16,128]{4,0,1,2,3:T(8,128)(2,1)} %bitcast.47), kind=kLoop, calls=%fused_computation.71 | loop fusion | flops 2097152 | bytes 16777216 | tf_op jit(solution)/shard_map/slice | solution.py:60
  419.9 14.4 %convolution_bitcast_fusion.1 = f32[16,1,16,128,128]{4,3,2,0,1:T(8,128)} fusion(bf16[64,2,16,16,128]{4,0,1,2,3:T(8,128)(2,1)} %copy.15, bf16[16,128,64,2,16]{1,2,3,4,0:T(8,128)(2,1)} %copy.11), kind=kOutput, calls=%fused_computation.10 | convolution fusion | flops 1073741824 | bytes 33554432 | tf_op jit(solution)/shard_map/sckbi,sckbj->bkij/dot_general | solution.py:61
  434.3 14.9 %convolution_bitcast_fusion = f32[16,1,16,128,128]{4,3,2,0,1:T(8,128)} fusion(bf16[64,2,16,16,128]{4,0,1,2,3:T(8,128)(2,1)} %copy.15, bf16[64,1,16,16,128]{4,0,1,2,3:T(8,128)(2,1)} %get-tuple-element.6, bf16[64,1,16,16,128]{4,0,1,2,3:T(8,128)(2,1)} %get-tuple-element.5), kind=kOutput, calls=%fused_computation.9 | convolution fusion | flops 1077936128 | bytes 33554432 | tf_op jit(solution)/shard_map/sckbi,sckbj->bkij/dot_general | solution.py:62
  449.2 12.2 %maximum_multiply_fusion = f32[16,2,16,128,128]{4,3,2,0,1:T(8,128)S(1)} fusion(f32[16,1,16,128,128]{4,3,2,0,1:T(8,128)} %convolution_bitcast_fusion, f32[16,1,16,128,128]{4,3,2,0,1:T(8,128)} %convolution_bitcast_fusion.1), kind=kLoop, calls=%fused_computation.3 | loop fusion | flops 16777216 | bytes 67108864 | tf_op jit(solution)/shard_map/div | solution.py:63
  461.4 0.0 copy-start.1
  461.4 11.3 %copy.17 = f32[16,2,16,128,128]{4,3,2,1,0:T(8,128)} copy(f32[16,2,16,128,128]{4,3,2,0,1:T(8,128)S(1)} %maximum_multiply_fusion) | data formatting | bytes 67108864 | tf_op jit(solution)/shard_map/div | solution.py:63
  472.7 0.0 copy-done.1
  (6 shorter events, 0.0 us)
Async XLA Ops:
  0.0 111.3 %copy-start = (s32[2048]{0:T(1024)S(1)}, s32[2048]{0:T(1024)}, u32[]{:S(2)}) copy-start(s32[2048]{0:T(1024)} %param.4) | copy-start | bytes 24580
  6.6 71.9 %collective-permute-start = (bf16[3,512,2048]{2,1,0:T(8,128)(2,1)}, bf16[3,512,2048]{2,1,0:T(8,128)(2,1)}, u32[]{:S(2)}, u32[]{:S(2)}) collective-permute-start(bf16[3,512,2048]{2,1,0:T(8,128)(2,1)} %bitcast), channel_id=1, source_target_pairs={{0,1},{1,2},{2,3},{3,4},{4,5},{5,6},{6,7},{7,8},{8,9},{9,10},{10,1... | collective-permute-start | bytes 18874376 | tf_op jit(solution)/shard_map/ppermute | solution.py:14
  95.6 15.5 %copy-start.2 = (s32[16,2]{0,1:T(2,128)S(1)}, s32[16,2]{0,1:T(2,128)}, u32[]{:S(2)}) copy-start(s32[16,2]{0,1:T(2,128)} %param.5) | copy-start | bytes 388
  103.9 189.6 %all-to-all-start = ((bf16[4,2,16,16,2048]{4,3,1,0,2:T(8,128)(2,1)}), bf16[4,2,16,16,2048]{4,3,1,0,2:T(8,128)(2,1)}, u32[]{:S(2)}, u32[]{:S(2)}) async-start(bf16[4,2,16,16,2048]{4,3,1,0,2:T(8,128)(2,1)} %copy.7), calls=%async_computation | async-start | bytes 16777216 | tf_op jit(solution)/shard_map/all_to_all | solution.py:56
  461.4 11.3 %copy-start.1 = (s32[2048]{0:T(1024)S(1)}, s32[2048]{0:T(1024)}, u32[]{:S(2)}) copy-start(s32[2048]{0:T(1024)} %param.4) | copy-start | bytes 24580
where the time goes:
time: 474 us; the launch traced here: 473 us
  waiting for transfers between devices  246 us (52%)
  local copies, waits for them, and re-layouts  148 us (31%)
  matrix products  46.3 us (10%)
  other arithmetic  20.9 us (4%)
  starting transfers between devices  10.9 us (2%)
    all_to_all x1, waiting for transfers between devices, body(): lax.all_to_all(spectra, 'tm', split_axis=2, concat_axis=0, tiled=True)  182 us
    ppermute x1, waiting for transfers between devices, from_behind(): return lax.ppermute(block, axis, route)  64.7 us
    gather x2, local copies, waits for them, and re-layouts, body(): second = data[:, :, :, columns[:, 1]]  46.9 us
    gather x2, local copies, waits for them, and re-layouts, body(): first = data[:, :, :, columns[:, 0]]  46.9 us
    squeeze x1, local copies, waits for them, and re-layouts, body(): lax.all_to_all(spectra, 'tm', split_axis=2, concat_axis=0, tiled=True)  26.8 us
    dot_general x1, matrix products, body(): jnp.einsum('kn,sni->ski', table, filtered, preferred_element_type=jnp.flo...  17.1 us
    dot_general x1, matrix products, body(): jnp.einsum('sckbi,sckbj->bkij', flipped, second, preferred_element_type=j...  14.9 us
    dot_general x1, matrix products, body(): jnp.einsum('sckbi,sckbj->bkij', first, second, preferred_element_type=jnp...  14.4 us
  transfers between devices with their start and end apart: 2, of which 2 were waited for; matrix products, arithmetic and copies ran while one was open for 1% of the time, Pallas kernels for 0%

commit v1 on v0

--- a/solution.py
+++ b/solution.py
@@ -6,6 +6,28 @@
 CHANNELS = 256
 TAPS = 4
 PANEL = 128
+
+
+def do_squares(inputs, out_dim, axis_k):
+    along_axis = "tm"
+    y2 = jax.lax.axis_size(along_axis)
+    w1 = jax.lax.axis_index(along_axis)
+    d_next, a_now = (y2, w1)
+    front = inputs.shape[out_dim] // d_next
+    mid_arr = list(inputs.shape)
+    mid_arr[out_dim] = front
+    low = mid_arr[axis_k]
+    mid_arr[axis_k] = low * d_next
+    step_out = jnp.zeros(mid_arr, inputs.dtype)
+    for num in range(d_next):
+        back = lax.dynamic_slice_in_dim(inputs, (a_now ^ num) * front, front, axis=out_dim)
+        if num:
+            clean = range(d_next)
+            arr_out = map(lambda d: (d, d ^ num), clean)
+            res = list(arr_out)
+            back = jax.lax.ppermute(back, along_axis, res)
+        step_out = lax.dynamic_update_slice_in_dim(step_out, back, (a_now ^ num) * low, axis=axis_k)
+    return step_out
 
 
 def from_behind(block, axis, distance):
@@ -53,7 +75,7 @@
     table = dft_table(CHANNELS)
     spectra = jnp.einsum("kn,sni->ski", table, filtered, preferred_element_type=jnp.float32)
     spectra = spectra.astype(jnp.bfloat16).reshape(spec_dev, 2, groups, band_dev, width)
-    data = lax.all_to_all(spectra, "tm", split_axis=2, concat_axis=0, tiled=True)[:, :, 0]
+    data = do_squares(spectra, 2, 0)[:, :, 0]
     total = data.shape[0]
     first = data[:, :, :, columns[:, 0]]
     second = data[:, :, :, columns[:, 1]]

time: 474 us -> 11200 us (23.63)
  local copies, waits for them, and re-layouts: 148 us -> 10900 us
    dynamic_update_slice x0 -> x16, local copies, waits for them, and re-layouts: none -> 10500 us  [do_squares(): lax.dynamic_update_slice_in_dim(step_out, back, (a_now ^ num) * low, axis...]
    ppermute x0 -> x15, local copies, waits for them, and re-layouts: none -> 258 us  [do_squares(): back = jax.lax.ppermute(back, along_axis, res)]
    all_to_all x1 -> x0, waiting for transfers between devices: 182 us -> none  [body(): lax.all_to_all(spectra, 'tm', split_axis=2, concat_axis=0, tiled=True)]
    ppermute x0 -> x15, waiting for transfers between devices: none -> 121 us  [do_squares(): back = jax.lax.ppermute(back, along_axis, res)]
  transfers between devices with their start and end apart: 2 -> 16, of which waited for: 2 -> 7; matrix products, arithmetic and copies ran while one was open for 1% -> 90% of each run, Pallas kernels for 0% -> 0%
where the time goes in v1:
time: 11200 us; the launch traced here: 11100 us
  local copies, waits for them, and re-layouts  10900 us (97%)
  waiting for transfers between devices  186 us (2%)
    dynamic_update_slice x16, local copies, waits for them, and re-layouts, do_squares(): lax.dynamic_update_slice_in_dim(step_out, back, (a_now ^ num) * low, axis...  10500 us
    ppermute x15, local copies, waits for them, and re-layouts, do_squares(): back = jax.lax.ppermute(back, along_axis, res)  258 us
  transfers between devices with their start and end apart: 16, of which 7 were waited for; matrix products, arithmetic and copies ran while one was open for 90% of the time, Pallas kernels for 0%

profile of v1, /device:TPU:13, one launch (start us, length us, event | category | flops | bytes accessed | tf_op | source)
XLA Modules:
  0.0 11140.5 jit_solution(15467728080952281660)
XLA Ops:
  14.0 64.5 collective-permute-done
  129.1 26.2 collective-permute-done.6
  169.2 46.1 collective-permute-done.9
  215.3 22.5 collective-permute-done.10
  262.6 684.8 %dynamic_update_slice.64 = bf16[64,2,16,2048]{0,2,3,1:T(8,128)(2,1)} dynamic-update-slice(bf16[64,2,16,2048]{0,2,3,1:T(8,128)(2,1)} %squeeze.42, bf16[4,2,16,2048]{0,2,3,1:T(8,128)(2,1)} %bitcast.59, s32[]{:T(128)S(6)} %select_n.167, s32[]{:T(128)} %constant.110.clone.1, s32[]{:T(128)} %constant.110.clone.1, s32[]{:T(128)} %constant.110.clone.1) | dynamic-update-slice | bytes 1048580 | tf_op jit(solution)/shard_map/dynamic_update_slice | solution.py:29
  964.1 684.8 %dynamic_update_slice.65 = bf16[64,2,16,2048]{0,2,3,1:T(8,128)(2,1)} dynamic-update-slice(bf16[64,2,16,2048]{0,2,3,1:T(8,128)(2,1)} %dynamic_update_slice.64, bf16[4,2,16,2048]{0,2,3,1:T(8,128)(2,1)} %bitcast.61, s32[]{:T(128)S(6)} %select_n.169, s32[]{:T(128)} %constant.110.clone.1, s32[]{:T(128)} %constant.110.clone.1, s32[]{:T(128)} %constant.110.clone.1) | dynamic-update-slice | bytes 1048580 | tf_op jit(solution)/shard_map/dynamic_update_slice | solution.py:29
  1665.7 684.7 %dynamic_update_slice.66 = bf16[64,2,16,2048]{0,2,3,1:T(8,128)(2,1)} dynamic-update-slice(bf16[64,2,16,2048]{0,2,3,1:T(8,128)(2,1)} %dynamic_update_slice.65, bf16[4,2,16,2048]{0,2,3,1:T(8,128)(2,1)} %bitcast.62, s32[]{:T(128)S(6)} %select_n.171, s32[]{:T(128)} %constant.110.clone.1, s32[]{:T(128)} %constant.110.clone.1, s32[]{:T(128)} %constant.110.clone.1) | dynamic-update-slice | bytes 1048580 | tf_op jit(solution)/shard_map/dynamic_update_slice | solution.py:29
  2367.2 684.7 %dynamic_update_slice.67 = bf16[64,2,16,2048]{0,2,3,1:T(8,128)(2,1)} dynamic-update-slice(bf16[64,2,16,2048]{0,2,3,1:T(8,128)(2,1)} %dynamic_update_slice.66, bf16[4,2,16,2048]{0,2,3,1:T(8,128)(2,1)} %bitcast.63, s32[]{:T(128)S(6)} %select_n.173, s32[]{:T(128)} %constant.110.clone.1, s32[]{:T(128)} %constant.110.clone.1, s32[]{:T(128)} %constant.110.clone.1) | dynamic-update-slice | bytes 1048580 | tf_op jit(solution)/shard_map/dynamic_update_slice | solution.py:29
  3068.6 684.7 %dynamic_update_slice.68 = bf16[64,2,16,2048]{0,2,3,1:T(8,128)(2,1)} dynamic-update-slice(bf16[64,2,16,2048]{0,2,3,1:T(8,128)(2,1)} %dynamic_update_slice.67, bf16[4,2,16,2048]{0,2,3,1:T(8,128)(2,1)} %bitcast.64, s32[]{:T(128)S(6)} %select_n.175, s32[]{:T(128)} %constant.110.clone.1, s32[]{:T(128)} %constant.110.clone.1, s32[]{:T(128)} %constant.110.clone.1) | dynamic-update-slice | bytes 1048580 | tf_op jit(solution)/shard_map/dynamic_update_slice | solution.py:29
  3770.3 684.7 %dynamic_update_slice.69 = bf16[64,2,16,2048]{0,2,3,1:T(8,128)(2,1)} dynamic-update-slice(bf16[64,2,16,2048]{0,2,3,1:T(8,128)(2,1)} %dynamic_update_slice.68, bf16[4,2,16,2048]{0,2,3,1:T(8,128)(2,1)} %bitcast.65, s32[]{:T(128)S(6)} %select_n.177, s32[]{:T(128)} %constant.110.clone.1, s32[]{:T(128)} %constant.110.clone.1, s32[]{:T(128)} %constant.110.clone.1) | dynamic-update-slice | bytes 1048580 | tf_op jit(solution)/shard_map/dynamic_update_slice | solution.py:29
  4471.7 684.7 %dynamic_update_slice.70 = bf16[64,2,16,2048]{0,2,3,1:T(8,128)(2,1)} dynamic-update-slice(bf16[64,2,16,2048]{0,2,3,1:T(8,128)(2,1)} %dynamic_update_slice.69, bf16[4,2,16,2048]{0,2,3,1:T(8,128)(2,1)} %bitcast.66, s32[]{:T(128)S(6)} %select_n.179, s32[]{:T(128)} %constant.110.clone.1, s32[]{:T(128)} %constant.110.clone.1, s32[]{:T(128)} %constant.110.clone.1) | dynamic-update-slice | bytes 1048580 | tf_op jit(solution)/shard_map/dynamic_update_slice | solution.py:29
  5173.2 195.9 %dynamic_update_slice.71 = bf16[64,2,16,2048]{0,2,3,1:T(8,128)(2,1)} dynamic-update-slice(bf16[64,2,16,2048]{0,2,3,1:T(8,128)(2,1)} %dynamic_update_slice.70, bf16[4,2,16,2048]{0,2,3,1:T(8,128)(2,1)} %bitcast.67, s32[]{:T(128)S(6)} %select_n.181, s32[]{:T(128)} %constant.110.clone.1, s32[]{:T(128)} %constant.110.clone.1, s32[]{:T(128)} %constant.110.clone.1) | dynamic-update-slice | bytes 1048580 | tf_op jit(solution)/shard_map/dynamic_update_slice | solution.py:29
  5369.2 17.5 copy.39
  5386.7 684.7 %dynamic_update_slice.72 = bf16[64,2,16,2048]{0,2,3,1:T(8,128)(2,1)} dynamic-update-slice(bf16[64,2,16,2048]{0,2,3,1:T(8,128)(2,1)} %dynamic_update_slice.71, bf16[4,2,16,2048]{0,2,3,1:T(8,128)(2,1)} %bitcast.68, s32[]{:T(128)S(6)} %select_n.183, s32[]{:T(128)} %constant.110.clone.1, s32[]{:T(128)} %constant.110.clone.1, s32[]{:T(128)} %constant.110.clone.1) | dynamic-update-slice | bytes 1048580 | tf_op jit(solution)/shard_map/dynamic_update_slice | solution.py:29
  6071.4 17.5 copy.40
  6088.9 684.7 %dynamic_update_slice.73 = bf16[64,2,16,2048]{0,2,3,1:T(8,128)(2,1)} dynamic-update-slice(bf16[64,2,16,2048]{0,2,3,1:T(8,128)(2,1)} %dynamic_update_slice.72, bf16[4,2,16,2048]{0,2,3,1:T(8,128)(2,1)} %bitcast.69, s32[]{:T(128)S(6)} %select_n.185, s32[]{:T(128)} %constant.110.clone.1, s32[]{:T(128)} %constant.110.clone.1, s32[]{:T(128)} %constant.110.clone.1) | dynamic-update-slice | bytes 1048580 | tf_op jit(solution)/shard_map/dynamic_update_slice | solution.py:29
  6773.7 17.5 copy.41
  6791.2 684.7 %dynamic_update_slice.74 = bf16[64,2,16,2048]{0,2,3,1:T(8,128)(2,1)} dynamic-update-slice(bf16[64,2,16,2048]{0,2,3,1:T(8,128)(2,1)} %dynamic_update_slice.73, bf16[4,2,16,2048]{0,2,3,1:T(8,128)(2,1)} %bitcast.70, s32[]{:T(128)S(6)} %select_n.187, s32[]{:T(128)} %constant.110.clone.1, s32[]{:T(128)} %constant.110.clone.1, s32[]{:T(128)} %constant.110.clone.1) | dynamic-update-slice | bytes 1048580 | tf_op jit(solution)/shard_map/dynamic_update_slice | solution.py:29
  7475.9 17.5 copy.42
  7493.5 684.7 %dynamic_update_slice.75 = bf16[64,2,16,2048]{0,2,3,1:T(8,128)(2,1)} dynamic-update-slice(bf16[64,2,16,2048]{0,2,3,1:T(8,128)(2,1)} %dynamic_update_slice.74, bf16[4,2,16,2048]{0,2,3,1:T(8,128)(2,1)} %bitcast.71, s32[]{:T(128)S(6)} %select_n.189, s32[]{:T(128)} %constant.110.clone.1, s32[]{:T(128)} %constant.110.clone.1, s32[]{:T(128)} %constant.110.clone.1) | dynamic-update-slice | bytes 1048580 | tf_op jit(solution)/shard_map/dynamic_update_slice | solution.py:29
  8178.2 17.5 copy.43
  8195.7 684.7 %dynamic_update_slice.76 = bf16[64,2,16,2048]{0,2,3,1:T(8,128)(2,1)} dynamic-update-slice(bf16[64,2,16,2048]{0,2,3,1:T(8,128)(2,1)} %dynamic_update_slice.75, bf16[4,2,16,2048]{0,2,3,1:T(8,128)(2,1)} %bitcast.72, s32[]{:T(128)S(6)} %select_n.191, s32[]{:T(128)} %constant.110.clone.1, s32[]{:T(128)} %constant.110.clone.1, s32[]{:T(128)} %constant.110.clone.1) | dynamic-update-slice | bytes 1048580 | tf_op jit(solution)/shard_map/dynamic_update_slice | solution.py:29
  8880.5 17.5 copy.44
  8898.0 684.7 %dynamic_update_slice.77 = bf16[64,2,16,2048]{0,2,3,1:T(8,128)(2,1)} dynamic-update-slice(bf16[64,2,16,2048]{0,2,3,1:T(8,128)(2,1)} %dynamic_update_slice.76, bf16[4,2,16,2048]{0,2,3,1:T(8,128)(2,1)} %bitcast.73, s32[]{:T(128)S(6)} %select_n.193, s32[]{:T(128)} %constant.110.clone.1, s32[]{:T(128)} %constant.110.clone.1, s32[]{:T(128)} %constant.110.clone.1) | dynamic-update-slice | bytes 1048580 | tf_op jit(solution)/shard_map/dynamic_update_slice | solution.py:29
  9582.8 17.7 copy.45
  9600.5 684.7 %dynamic_update_slice.78 = bf16[64,2,16,2048]{0,2,3,1:T(8,128)(2,1)} dynamic-update-slice(bf16[64,2,16,2048]{0,2,3,1:T(8,128)(2,1)} %dynamic_update_slice.77, bf16[4,2,16,2048]{0,2,3,1:T(8,128)(2,1)} %bitcast.74, s32[]{:T(128)S(6)} %select_n.195, s32[]{:T(128)} %constant.110.clone.1, s32[]{:T(128)} %constant.110.clone.1, s32[]{:T(128)} %constant.110.clone.1) | dynamic-update-slice | bytes 1048580 | tf_op jit(solution)/shard_map/dynamic_update_slice | solution.py:29
  10285.2 17.5 copy.46
  10302.8 684.7 %dynamic_update_slice.79 = bf16[64,2,16,2048]{0,2,3,1:T(8,128)(2,1)} dynamic-update-slice(bf16[64,2,16,2048]{0,2,3,1:T(8,128)(2,1)} %dynamic_update_slice.78, bf16[4,2,16,2048]{0,2,3,1:T(8,128)(2,1)} %bitcast.60, s32[]{:T(128)S(6)} %select_n.197, s32[]{:T(128)} %constant.110.clone.1, s32[]{:T(128)} %constant.110.clone.1, s32[]{:T(128)} %constant.110.clone.1) | dynamic-update-slice | bytes 1048580 | tf_op jit(solution)/shard_map/dynamic_update_slice | solution.py:29
  10987.5 25.9 gather_fusion.1
  11013.4 21.1 copy.49
  11034.5 25.9 gather_fusion.2
  11060.4 21.0 copy.52
  (75 shorter events, 278.3 us)
Async XLA Ops:
  0.0 128.5 %copy-start = (s32[2048]{0:T(1024)S(1)}, s32[2048]{0:T(1024)}, u32[]{:S(2)}) copy-start(s32[2048]{0:T(1024)} %param.4) | copy-start | bytes 24580
  6.6 71.9 collective-permute-start
  93.5 34.8 copy-start.8
  96.1 4.9 collective-permute-start.1
  97.4 13.6 collective-permute-start.2
  98.6 24.1 collective-permute-start.3
  99.1 25.9 collective-permute-start.4
  99.2 25.9 collective-permute-start.5
  100.9 0.8 copy-start.4
  101.7 53.6 collective-permute-start.6
  111.0 14.2 copy-start.2
  111.0 55.5 collective-permute-start.7
  122.6 44.1 collective-permute-start.8
  124.9 90.4 collective-permute-start.9
  125.1 112.6 %collective-permute-start.10 = (bf16[4,2,1,16,2048]{4,3,2,1,0:T(8,128)(2,1)}, bf16[4,2,1,16,2048]{4,3,2,1,0:T(8,128)(2,1)}, u32[]{:S(2)}, u32[]{:S(2)}) collective-permute-start(bf16[4,2,1,16,2048]{4,3,2,1,0:T(8,128)(2,1)} %get-tuple-element.12), channel_id=1, source_target_pairs={{0,10},{1,11},{2,8},{3,9},{4,14},{5,15},{6,12},{7,13},{8,2},{9,3},... | collective-permute-start | bytes 1572872 | tf_op jit(solution)/shard_map/ppermute | solution.py:28
  155.3 7320.7 %collective-permute-start.11 = (bf16[4,2,1,16,2048]{4,3,2,1,0:T(8,128)(2,1)}, bf16[4,2,1,16,2048]{4,3,2,1,0:T(8,128)(2,1)}, u32[]{:S(2)}, u32[]{:S(2)}) collective-permute-start(bf16[4,2,1,16,2048]{4,3,2,1,0:T(8,128)(2,1)} %get-tuple-element.11), channel_id=1, source_target_pairs={{0,11},{1,10},{2,9},{3,8},{4,15},{5,14},{6,13},{7,12},{8,3},{9,2},... | collective-permute-start | bytes 1572872 | tf_op jit(solution)/shard_map/ppermute | solution.py:28
  166.5 8011.7 %collective-permute-start.12 = (bf16[4,2,1,16,2048]{4,3,2,1,0:T(8,128)(2,1)}, bf16[4,2,1,16,2048]{4,3,2,1,0:T(8,128)(2,1)}, u32[]{:S(2)}, u32[]{:S(2)}) collective-permute-start(bf16[4,2,1,16,2048]{4,3,2,1,0:T(8,128)(2,1)} %get-tuple-element.10), channel_id=1, source_target_pairs={{0,12},{1,13},{2,14},{3,15},{4,8},{5,9},{6,10},{7,11},{8,4},{9,5},... | collective-permute-start | bytes 1572872 | tf_op jit(solution)/shard_map/ppermute | solution.py:28
  166.7 8713.8 %collective-permute-start.13 = (bf16[4,2,1,16,2048]{4,3,2,1,0:T(8,128)(2,1)}, bf16[4,2,1,16,2048]{4,3,2,1,0:T(8,128)(2,1)}, u32[]{:S(2)}, u32[]{:S(2)}) collective-permute-start(bf16[4,2,1,16,2048]{4,3,2,1,0:T(8,128)(2,1)} %get-tuple-element.9), channel_id=1, source_target_pairs={{0,13},{1,12},{2,15},{3,14},{4,9},{5,8},{6,11},{7,10},{8,5},{9,4},... | collective-permute-start | bytes 1572872 | tf_op jit(solution)/shard_map/ppermute | solution.py:28
  215.3 9367.5 %collective-permute-start.14 = (bf16[4,2,1,16,2048]{4,3,2,1,0:T(8,128)(2,1)}, bf16[4,2,1,16,2048]{4,3,2,1,0:T(8,128)(2,1)}, u32[]{:S(2)}, u32[]{:S(2)}) collective-permute-start(bf16[4,2,1,16,2048]{4,3,2,1,0:T(8,128)(2,1)} %get-tuple-element.8), channel_id=1, source_target_pairs={{0,14},{1,15},{2,12},{3,13},{4,10},{5,11},{6,8},{7,9},{8,6},{9,7},... | collective-permute-start | bytes 1572872 | tf_op jit(solution)/shard_map/ppermute | solution.py:28
  237.8 10047.5 %collective-permute-start.15 = (bf16[4,2,1,16,2048]{4,3,2,1,0:T(8,128)(2,1)}, bf16[4,2,1,16,2048]{4,3,2,1,0:T(8,128)(2,1)}, u32[]{:S(2)}, u32[]{:S(2)}) collective-permute-start(bf16[4,2,1,16,2048]{4,3,2,1,0:T(8,128)(2,1)} %get-tuple-element.7), channel_id=1, source_target_pairs={{0,15},{1,14},{2,13},{3,12},{4,11},{5,10},{6,9},{7,8},{8,7},{9,6},... | collective-permute-start | bytes 1572872 | tf_op jit(solution)/shard_map/ppermute | solution.py:28
  262.6 684.8 %copy-start.5 = (bf16[4,2,1,16,2048]{4,3,2,1,0:T(8,128)(2,1)S(1)}, bf16[4,2,1,16,2048]{4,3,2,1,0:T(8,128)(2,1)}, u32[]{:S(2)}) copy-start(bf16[4,2,1,16,2048]{4,3,2,1,0:T(8,128)(2,1)} %copy-done.4) | copy-start | bytes 1572868
  964.1 684.8 %copy-start.3 = (bf16[4,2,1,16,2048]{4,3,2,1,0:T(8,128)(2,1)S(1)}, bf16[4,2,1,16,2048]{4,3,2,1,0:T(8,128)(2,1)}, u32[]{:S(2)}) copy-start(bf16[4,2,1,16,2048]{4,3,2,1,0:T(8,128)(2,1)} %copy-done.2) | copy-start | bytes 1572868
  10302.8 684.8 %copy-start.7 = (s32[2048]{0:T(1024)S(1)}, s32[2048]{0:T(1024)}, u32[]{:S(2)}) copy-start(s32[2048]{0:T(1024)} %fusion.24) | copy-start | bytes 24580
  11013.4 21.1 copy-start.6
  11128.8 11.3 copy-start.1
